TPU v7x, 32 devices: a whole 2x2x4 slice. The times are simulated.
32 devices in a mesh: scene: 2 (over y), tok: 8 (over z, x), hid: 2 (over core).
Axes of the slice: x: 2, y: 2, z: 4, core: 2. Of those that a mesh axis runs over, the one named last changes fastest.
Arguments:
- input_keys: bfloat16 [16384, 384], P(('scene', 'tok'), 'hid'), parts along dimension 0, may hold values from -6 to 6
- input_values: bfloat16 [16384, 384], P(('scene', 'tok'), 'hid'), parts along dimension 0, may hold values from -6 to 6
- input_lr: float32 [16384], P(('scene', 'tok')), parts along dimension 0, may hold values from 0.1 to 1
- gate_weight: bfloat16 [384, 1536], P('tok', 'hid'), may hold values from -0.3125 to 0.3125
- up_weight: bfloat16 [384, 1536], P('tok', 'hid'), may hold values from -0.3125 to 0.3125
- down_weight: bfloat16 [384, 1536], P('tok', 'hid'), may hold values from -0.15625 to 0.15625
- queries: bfloat16 [2048, 384], P(('scene', 'tok'), 'hid'), parts along dimension 0, may hold values from -6 to 6
- out_grad: bfloat16 [2048, 384], P(('scene', 'tok'), 'hid'), parts along dimension 0, may hold values from -6 to 6
Outputs:
- target_out: bfloat16 [2048, 384], P(('scene', 'tok'), 'hid'), parts along dimension 0
- query_grad: bfloat16 [2048, 384], P(('scene', 'tok'), 'hid'), parts along dimension 0
There are 2 independent parts, one for each index of `scene`. A program takes and returns all parts, laid end to end along the dimension named above; an argument that names none is the same for every part. Nothing has to cross between parts.
All inputs are finite; a program needn't handle non-finite values.
Results may differ from a plain program's by a relative error of at most 0.009.
Values may be sent and summed in bfloat16 or wider, within the bound.
A program may use at most 64 MiB of HBM per device.

v0:
```python
import jax
import jax.numpy as jnp
from jax import lax
from jax.sharding import PartitionSpec as P

HID = 1536
step_ratio = 0.5
epsilon = 1e-06


def silu_slope(pre):
    sigma = jax.nn.sigmoid(pre)
    return sigma * (1.0 + pre * (1.0 - sigma))


def contract_rows(left, right):
    return lax.dot_general(
        left, right, (((0,), (0,)), ((), ())), preferred_element_type=jnp.float32
    )


def contract_cols(left, right):
    return lax.dot_general(
        left, right, (((1,), (1,)), ((), ())), preferred_element_type=jnp.float32
    )


def finish(moved, wsq, msq):
    return (moved * (jnp.sqrt(wsq) / jnp.sqrt(msq + epsilon))[:, None]).astype(jnp.bfloat16)


def shards(
    input_keys, input_values, input_lr, gate_weight, up_weight, down_weight, queries, out_grad
):
    keys, values = (
        lax.all_gather(input_keys, "hid", axis=1, tiled=True),
        lax.all_gather(input_values, "hid", axis=1, tiled=True),
    )
    w_gate, w_up, w_down = (
        lax.all_gather(gate_weight, "tok", axis=0, tiled=True),
        lax.all_gather(up_weight, "tok", axis=0, tiled=True),
        lax.all_gather(down_weight, "tok", axis=0, tiled=True),
    )
    scaled = (input_lr[:, None] * values.astype(jnp.float32)).astype(jnp.bfloat16)
    key_gate = jnp.dot(keys, w_gate, preferred_element_type=jnp.float32)
    key_up = jnp.dot(keys, w_up, preferred_element_type=jnp.float32)
    gate_act = jax.nn.silu(key_gate)
    key_act = (gate_act * key_up).astype(jnp.bfloat16)
    back = jnp.dot(scaled, w_down, preferred_element_type=jnp.float32)
    d_gate = (-back * key_up * silu_slope(key_gate)).astype(jnp.bfloat16)
    d_up = (-back * gate_act).astype(jnp.bfloat16)
    width = gate_weight.shape[1]
    grads = lax.psum(
        jnp.concatenate(
            [
                contract_rows(keys, d_gate),
                contract_rows(keys, d_up),
                -contract_rows(scaled, key_act),
            ],
            axis=1,
        ),
        "tok",
    )
    olds = (w_gate, w_up, w_down)
    pieces = [grads[:, :width], grads[:, width : 2 * width], grads[:, 2 * width :]]
    weights = [old.astype(jnp.float32) for old in olds]
    renewed = []
    stats = []
    for weight, grad in zip(weights, pieces):
        stats.append(jnp.sum(weight * weight, axis=1))
        stats.append(jnp.sum(weight * grad, axis=1))
        stats.append(jnp.sum(grad * grad, axis=1))
    totals = lax.psum(
        (stats[0], stats[1], stats[2], stats[3], stats[4], stats[5], stats[6], stats[7], stats[8]),
        "hid",
    )
    for index in range(3):
        wsq = totals[3 * index] / HID
        cross = totals[3 * index + 1] / HID
        gsq = totals[3 * index + 2] / HID
        scale = step_ratio * jnp.sqrt(wsq) / jnp.sqrt(gsq + epsilon)
        moved = weights[index] - scale[:, None] * pieces[index]
        msq = wsq - 2.0 * scale * cross + scale * scale * gsq
        renewed.append(finish(moved, wsq, msq))
    new_gate, new_up, new_down = (renewed[0], renewed[1], renewed[2])
    query_rows, grad_rows = (
        lax.all_gather(queries, "hid", axis=1, tiled=True),
        lax.all_gather(out_grad, "hid", axis=1, tiled=True),
    )
    query_gate = jnp.dot(query_rows, new_gate, preferred_element_type=jnp.float32)
    query_up = jnp.dot(query_rows, new_up, preferred_element_type=jnp.float32)
    query_silu = jax.nn.silu(query_gate)
    query_act = (query_silu * query_up).astype(jnp.bfloat16)
    out_part = contract_cols(query_act, new_down)
    query_back = jnp.dot(grad_rows, new_down, preferred_element_type=jnp.float32)
    q_gate_grad = (query_back * query_up * silu_slope(query_gate)).astype(jnp.bfloat16)
    q_up_grad = (query_back * query_silu).astype(jnp.bfloat16)
    grad_part = contract_cols(q_gate_grad, new_gate) + contract_cols(q_up_grad, new_up)
    out_sum, grad_sum = (
        lax.psum_scatter(
            out_part.astype(jnp.bfloat16), "hid", scatter_dimension=1, tiled=True
        ).astype(jnp.float32),
        lax.psum_scatter(
            grad_part.astype(jnp.bfloat16), "hid", scatter_dimension=1, tiled=True
        ).astype(jnp.float32),
    )
    return (out_sum.astype(jnp.bfloat16), grad_sum.astype(jnp.bfloat16))


def solution(mesh):
    return jax.shard_map(
        shards,
        mesh=mesh,
        in_specs=(
            P(("scene", "tok"), "hid"),
            P(("scene", "tok"), "hid"),
            P(("scene", "tok")),
            P("tok", "hid"),
            P("tok", "hid"),
            P("tok", "hid"),
            P(("scene", "tok"), "hid"),
            P(("scene", "tok"), "hid"),
        ),
        out_specs=(P(("scene", "tok"), "hid"), P(("scene", "tok"), "hid")),
        check_vma=False,
    )
```

profile of v0, /device:TPU:0, one launch (start us, length us, event | category | flops | bytes accessed | tf_op | source)
XLA Modules:
  0.0 297.7 jit_solution(15559393787212214560)
XLA Ops:
  7.2 0.0 copy-start.6
  7.2 0.0 all-reduce.3.cloned.1.call-start
  7.2 2.7 all_gather.24
  9.9 33.4 %all_gather.21 = bf16[384,768]{1,0:T(8,128)(2,1)S(1)} all-gather(bf16[48,768]{1,0:T(8,128)(2,1)} %param.11), channel_id=1, replica_groups=mesh['scene'=2,'tok'=8,'hid'=2] {'tok'}, dimensions={0}, use_global_device_ids=true | all-gather | bytes 663552 | tf_op jit(solution)/shard_map/all_gather | solution.py:40
  43.4 0.0 copy-done.6
  43.4 31.3 %all_gather.25 = bf16[384,768]{1,0:T(8,128)(2,1)S(1)} all-gather(bf16[48,768]{1,0:T(8,128)(2,1)S(1)} %copy-done.6), channel_id=1, replica_groups=mesh['scene'=2,'tok'=8,'hid'=2] {'tok'}, dimensions={0}, use_global_device_ids=true | all-gather | bytes 663552 | tf_op jit(solution)/shard_map/all_gather | solution.py:41
  74.6 1.0 fusion.34
  75.7 0.0 copy-start.5
  75.7 0.0 copy-start.7
  75.7 1.0 fusion.33
  76.7 0.0 copy-done.5
  76.7 0.0 copy-start.10
  76.7 2.4 all_gather.22
  79.1 0.0 copy-done.7
  79.1 31.4 %all_gather.23 = bf16[384,768]{1,0:T(8,128)(2,1)S(1)} all-gather(bf16[48,768]{1,0:T(8,128)(2,1)S(1)} %copy-done.7), channel_id=1, replica_groups=mesh['scene'=2,'tok'=8,'hid'=2] {'tok'}, dimensions={0}, use_global_device_ids=true | all-gather | bytes 663552 | tf_op jit(solution)/shard_map/all_gather | solution.py:42
  110.5 0.0 copy-done.10
  110.5 1.0 fusion.20
  111.6 1.2 fusion.6
  112.8 1.5 fusion.4
  114.3 1.3 fusion.5
  115.6 2.0 pad_maximum_fusion
  117.6 0.0 all-reduce.3.cloned.1.call-update
  117.7 0.0 copy-start.8
  117.7 0.0 copy-start.9
  117.7 0.0 reduce-scatter.5.cloned.1.call-start
  117.7 1.1 copy.14
  118.8 1.1 copy.16
  119.8 1.1 copy.17
  121.0 0.0 copy-done.8
  121.0 2.0 all_gather.27
  123.0 0.0 copy-done.9
  123.0 2.0 all_gather.26
  125.0 132.9 %all-reduce.3.cloned.1.call-done = f32[384,2304]{0,1:T(8,128)} async-done(((f32[384,2304]{0,1:T(8,128)}), f32[384,2304]{0,1:T(8,128)}) %all-reduce.3.cloned.1.call-update) | async-done | bytes 3538960 | tf_op jit(solution)/shard_map/psum | solution.py:53
  257.8 0.0 copy-start
  257.9 4.1 %multiply_reduce_fusion.2 = (f32[384]{0:T(512)S(1)}, f32[384]{0:T(512)S(1)}, f32[384]{0:T(512)S(1)}, f32[384]{0:T(512)S(1)}, f32[384]{0:T(512)}, /*index=5*/f32[...) fusion(f32[384,2304]{0,1:T(8,128)} %all-reduce.3.cloned.1.call-done, bf16[384,768]{0,1:T(8,128)(2,1)} %copy.14, ...), kind=kLoop, calls=%fused_computation.39 | loop fusion | flops 6189696 | bytes 5322240 | tf_op jit(solution)/shard_map/reduce_sum | solution.py:72
  261.9 4.6 %all-reduce = (f32[384]{0:T(512)}, f32[384]{0:T(512)}, f32[384]{0:T(512)}, f32[384]{0:T(512)}, f32[384]{0:T(512)}, /*index=5*/f32[384]{0:T(512)}, f32[384]{0:T(512)}, f32[384]{0:T(512)}, f32[384]{0:T(512)}) all-reduce(f32[384]{0:T(512)S(1)} %get-tuple-element.5, ...), channel_id=1, replica_groups=mesh['scene'=2,'tok'=8,'hid'=2] {'hid'}, use_global_device_ids=true, to_apply=%region_18.19 | all-reduce | flops 3456 | bytes 27648 | tf_op jit(solution)/shard_map/psum | solution.py:73
  266.5 0.7 rsqrt_multiply_fusion.5
  267.2 0.8 rsqrt_multiply_fusion.1
  268.0 0.0 copy-done
  268.0 0.0 copy-start.3
  268.0 2.0 fusion.9
  270.0 0.0 copy-start.1
  270.1 0.0 copy-start.4
  270.1 0.0 copy-done.3
  270.1 0.3 convolution_bitcast_fusion.1
  270.4 0.3 convolution_bitcast_fusion.2
  270.7 0.3 copy-done.4
  271.0 0.3 convolution_bitcast_fusion
  271.4 0.0 copy-done.1
  271.4 0.5 fusion.24
  271.8 0.0 copy-start.2
  271.8 1.1 fusion.19
  272.9 0.0 reduce-scatter.5.cloned.1.call-update
  272.9 0.0 reduce-scatter.3.cloned.1.call-start
  273.0 0.0 copy-done.2
  273.0 1.0 convolution_convert_fusion
  274.0 0.0 reduce-scatter.3.cloned.1.call-update
  274.0 5.6 %reduce-scatter.5.cloned.1.call-done = bf16[128,192]{0,1:T(8,128)(2,1)} async-done(((bf16[128,384]{0,1:T(8,128)(2,1)}), bf16[128,192]{0,1:T(8,128)(2,1)}) %reduce-scatter.5.cloned.1.call-update) | async-done | bytes 49168 | tf_op jit(solution)/shard_map/reduce_scatter | solution.py:103
  279.7 11.5 %reduce-scatter.3.cloned.1.call-done = bf16[128,192]{0,1:T(8,128)(2,1)} async-done(((bf16[128,384]{0,1:T(8,128)(2,1)}), bf16[128,192]{0,1:T(8,128)(2,1)}) %reduce-scatter.3.cloned.1.call-update) | async-done | bytes 49168 | tf_op jit(solution)/shard_map/reduce_scatter | solution.py:100
Async XLA Ops:
  7.2 36.2 %copy-start.6 = (bf16[48,768]{1,0:T(8,128)(2,1)S(1)}, bf16[48,768]{1,0:T(8,128)(2,1)}, u32[]{:S(2)}) copy-start(bf16[48,768]{1,0:T(8,128)(2,1)} %param.12) | copy-start | bytes 221188
  7.2 250.7 %all-reduce.3.cloned.1.call-start = ((), (), s32[]{:S(2)}) async-start(), calls=%async_computation.2 | async-start | bytes 7077888 | tf_op jit(solution)/shard_map/psum | solution.py:53
  75.7 1.1 copy-start.5
  75.7 3.4 %copy-start.7 = (bf16[48,768]{1,0:T(8,128)(2,1)S(1)}, bf16[48,768]{1,0:T(8,128)(2,1)}, u32[]{:S(2)}) copy-start(bf16[48,768]{1,0:T(8,128)(2,1)} %param.13) | copy-start | bytes 221188
  76.7 33.8 %copy-start.10 = (f32[1024]{0:T(1024)S(1)}, f32[1024]{0:T(1024)}, u32[]{:S(2)}) copy-start(f32[1024]{0:T(1024)} %param.10) | copy-start | bytes 12292
  117.7 3.3 %copy-start.8 = (bf16[128,192]{0,1:T(8,128)(2,1)S(1)}, bf16[128,192]{0,1:T(8,128)(2,1)}, u32[]{:S(2)}) copy-start(bf16[128,192]{0,1:T(8,128)(2,1)} %param.15) | copy-start | bytes 147460
  117.7 5.3 %copy-start.9 = (bf16[128,192]{0,1:T(8,128)(2,1)S(1)}, bf16[128,192]{0,1:T(8,128)(2,1)}, u32[]{:S(2)}) copy-start(bf16[128,192]{0,1:T(8,128)(2,1)} %param.14) | copy-start | bytes 147460
  117.7 162.0 %reduce-scatter.5.cloned.1.call-start = ((), (), s32[]{:S(2)}) async-start(), calls=%async_computation.4 | async-start | bytes 147456 | tf_op jit(solution)/shard_map/reduce_scatter | solution.py:103
  257.8 10.2 %copy-start = (f32[384,2304]{0,1:T(8,128)S(1)}, f32[384,2304]{0,1:T(8,128)}, u32[]{:S(2)}) copy-start(f32[384,2304]{0,1:T(8,128)} %all-reduce.3.cloned.1.call-done) | copy-start | bytes 10616836
  268.0 2.1 copy-start.3
  270.0 1.3 copy-start.1
  270.1 1.0 copy-start.4
  271.8 1.2 copy-start.2
  272.9 18.2 %reduce-scatter.3.cloned.1.call-start = ((), (), s32[]{:S(2)}) async-start(), calls=%async_computation.3 | async-start | bytes 147456 | tf_op jit(solution)/shard_map/reduce_scatter | solution.py:100
Sparse Core Ops, SparseCore 0:
  117.8 140.0 all-reduce.2
  273.1 6.5 reduce-scatter.4
  282.5 8.6 reduce-scatter.2
where the time goes:
time: 298 us
  waiting for transfers between devices  150 us (50%)
  blocking collectives  110 us (37%)
  between operations  13.9 us (5%)
  matrix products  10.6 us (4%)
  other arithmetic  9.59 us (3%)
  local copies, waits for them, and re-layouts  3.61 us (1%)
    psum x1, waiting for transfers between devices, shards(): lax.psum(jnp.concatenate([contract_rows(keys, d_gate), contract_rows(keys...  133 us
    all_gather x1, blocking collectives, shards(): lax.all_gather(gate_weight, 'tok', axis=0, tiled=True)  33.4 us
    all_gather x1, blocking collectives, shards(): lax.all_gather(down_weight, 'tok', axis=0, tiled=True)  31.4 us
    all_gather x1, blocking collectives, shards(): lax.all_gather(up_weight, 'tok', axis=0, tiled=True)  31.3 us
    reduce_scatter x1, waiting for transfers between devices, shards(): lax.psum_scatter(out_part.astype(jnp.bfloat16), 'hid', scatter_dimension=...  11.5 us
  transfers between devices with their start and end apart: 3, of which 3 were waited for; matrix products, arithmetic and copies ran while one was open for 1% of the time, Pallas kernels for 0%

commit v1 on v0

--- a/solution.py
+++ b/solution.py
@@ -50,17 +50,12 @@
     d_gate = (-back * key_up * silu_slope(key_gate)).astype(jnp.bfloat16)
     d_up = (-back * gate_act).astype(jnp.bfloat16)
     width = gate_weight.shape[1]
-    grads = lax.psum(
-        jnp.concatenate(
-            [
-                contract_rows(keys, d_gate),
-                contract_rows(keys, d_up),
-                -contract_rows(scaled, key_act),
-            ],
-            axis=1,
-        ),
-        "tok",
+    block = jnp.concatenate(
+        [contract_rows(keys, d_gate), contract_rows(keys, d_up), -contract_rows(scaled, key_act)],
+        axis=1,
     )
+    parts = lax.all_gather(block, "tok")
+    grads = jnp.sum(parts, axis=0)
     olds = (w_gate, w_up, w_down)
     pieces = [grads[:, :width], grads[:, width : 2 * width], grads[:, 2 * width :]]
     weights = [old.astype(jnp.float32) for old in olds]

time: 298 us -> 749 us (2.51)
  waiting for transfers between devices: 150 us -> 551 us
  other arithmetic: 9.59 us -> 43.5 us
  local copies, waits for them, and re-layouts: 3.61 us -> 18.4 us
    all_gather x0 -> x1, waiting for transfers between devices: none -> 533 us  [shards(): parts = lax.all_gather(block, 'tok')]
    psum x1 -> x0, waiting for transfers between devices: 133 us -> none  [shards(): lax.psum(jnp.concatenate([contract_rows(keys, d_gate), contract_rows(keys...]
    reduce_sum x0 -> x1, other arithmetic: none -> 36.4 us  [shards(): grads = jnp.sum(parts, axis=0)]
    unnamed x22 -> x25, local copies, waits for them, and re-layouts: 0.38 us -> 15.2 us
where the time goes in v1:
time: 749 us; the launch traced here: 748 us
  waiting for transfers between devices  551 us (74%)
  blocking collectives  111 us (15%)
  other arithmetic  43.5 us (6%)
  local copies, waits for them, and re-layouts  18.4 us (2%)
  between operations  14 us (2%)
  matrix products  10.5 us (1%)
    all_gather x1, waiting for transfers between devices, shards(): parts = lax.all_gather(block, 'tok')  533 us
    reduce_sum x1, other arithmetic, shards(): grads = jnp.sum(parts, axis=0)  36.4 us
    all_gather x1, blocking collectives, shards(): lax.all_gather(gate_weight, 'tok', axis=0, tiled=True)  33.4 us
    all_gather x1, blocking collectives, shards(): lax.all_gather(down_weight, 'tok', axis=0, tiled=True)  31.7 us
    all_gather x1, blocking collectives, shards(): lax.all_gather(up_weight, 'tok', axis=0, tiled=True)  31.5 us
    unnamed x25, local copies, waits for them, and re-layouts  15.2 us
  transfers between devices with their start and end apart: 3, of which 3 were waited for; matrix products, arithmetic and copies ran while one was open for 1% of the time, Pallas kernels for 0%

profile of v1, /device:TPU:0, one launch (start us, length us, event | category | flops | bytes accessed | tf_op | source)
XLA Modules:
  0.0 748.2 jit_solution(9852515682568368971)
XLA Ops:
  7.2 0.0 all-gather.3.cloned.1.call-start
  7.2 2.7 all_gather.30
  9.9 33.4 %all_gather.27 = bf16[384,768]{1,0:T(8,128)(2,1)S(1)} all-gather(bf16[48,768]{1,0:T(8,128)(2,1)} %param.11), channel_id=1, replica_groups=mesh['scene'=2,'tok'=8,'hid'=2] {'tok'}, dimensions={0}, use_global_device_ids=true | all-gather | bytes 663552 | tf_op jit(solution)/shard_map/all_gather | solution.py:40
  43.3 31.5 %all_gather.31 = bf16[384,768]{1,0:T(8,128)(2,1)S(1)} all-gather(bf16[48,768]{1,0:T(8,128)(2,1)} %param.12), channel_id=1, replica_groups=mesh['scene'=2,'tok'=8,'hid'=2] {'tok'}, dimensions={0}, use_global_device_ids=true | all-gather | bytes 663552 | tf_op jit(solution)/shard_map/all_gather | solution.py:41
  74.8 1.0 fusion.34
  75.9 0.0 copy-start.7
  75.9 0.0 copy-start.8
  75.9 0.0 copy-start.11
  75.9 1.0 fusion.33
  76.9 0.0 copy-done.7
  76.9 2.4 all_gather.28
  79.3 0.0 copy-done.8
  79.3 31.7 %all_gather.29 = bf16[384,768]{1,0:T(8,128)(2,1)S(1)} all-gather(bf16[48,768]{1,0:T(8,128)(2,1)S(1)} %copy-done.8), channel_id=1, replica_groups=mesh['scene'=2,'tok'=8,'hid'=2] {'tok'}, dimensions={0}, use_global_device_ids=true | all-gather | bytes 663552 | tf_op jit(solution)/shard_map/all_gather | solution.py:42
  111.1 0.0 copy-done.11
  111.1 1.0 fusion.20
  112.1 1.2 fusion.6
  113.3 1.5 fusion.4
  114.8 1.3 fusion.5
  116.1 2.1 pad_maximum_fusion
  118.2 0.0 copy-start.9
  118.2 0.0 copy-start.10
  118.2 0.0 all-gather.3.cloned.1.call-update
  118.2 0.0 reduce-scatter.5.cloned.1.call-start
  118.3 1.1 copy.15
  119.3 1.1 copy.17
  120.4 1.1 copy.18
  121.5 0.0 copy-done.9
  121.5 2.0 all_gather.35
  123.5 0.0 copy-done.10
  123.5 2.2 all_gather.34
  125.6 533.0 %all-gather.3.cloned.1.call-done = f32[3072,2304]{0,1:T(8,128)} async-done(((f32[384,2304]{0,1:T(8,128)}), f32[3072,2304]{0,1:T(8,128)}) %all-gather.3.cloned.1.call-update) | async-done | bytes 28311568 | tf_op jit(solution)/shard_map/all_gather | solution.py:57
  658.7 15.0 %copy.20 = f32[288,8,8,384]{3,2,1,0:T(8,128)S(1)} copy(f32[288,8,8,384]{3,1,2,0:T(8,128)} %bitcast.31) | data formatting | bytes 56623104
  673.7 0.0 copy-start
  673.7 0.0 copy-start.1
  673.7 0.0 copy-start.2
  673.7 36.4 %bitcast_reduce_fusion = f32[384,2304]{0,1:T(8,128)S(1)} fusion(f32[288,8,8,384]{3,2,1,0:T(8,128)S(1)} %copy.20), kind=kLoop, calls=%fused_computation | loop fusion | flops 6193152 | bytes 31850496 | tf_op jit(solution)/shard_map/reduce_sum | solution.py:58
  710.1 0.0 copy-done
  710.1 0.0 copy-done.1
  710.2 0.0 copy-done.2
  710.2 1.5 multiply_reduce_fusion.2
  711.6 4.6 all-reduce
  716.2 0.7 rsqrt_multiply_fusion.5
  716.9 0.8 rsqrt_multiply_fusion.1
  717.7 0.0 copy-start.5
  717.7 0.0 copy-start.6
  717.7 2.0 fusion.9
  719.8 0.0 copy-start.3
  719.8 0.0 copy-done.5
  719.8 0.3 convolution_bitcast_fusion.1
  720.1 0.3 convolution_bitcast_fusion.2
  720.4 0.2 copy-done.3
  720.6 0.0 copy-done.6
  720.6 0.3 convolution_bitcast_fusion
  720.9 0.0 copy-start.4
  720.9 0.5 fusion.24
  721.4 1.1 fusion.19
  722.4 0.0 reduce-scatter.5.cloned.1.call-update
  722.4 0.0 reduce-scatter.3.cloned.1.call-start
  722.5 0.0 copy-done.4
  722.5 1.0 convolution_convert_fusion
  723.5 0.0 reduce-scatter.3.cloned.1.call-update
  723.6 6.6 reduce-scatter.5.cloned.1.call-done
  730.1 11.5 %reduce-scatter.3.cloned.1.call-done = bf16[128,192]{0,1:T(8,128)(2,1)} async-done(((bf16[128,384]{0,1:T(8,128)(2,1)}), bf16[128,192]{0,1:T(8,128)(2,1)}) %reduce-scatter.3.cloned.1.call-update) | async-done | bytes 49168 | tf_op jit(solution)/shard_map/reduce_scatter | solution.py:95
Async XLA Ops:
  7.2 651.5 %all-gather.3.cloned.1.call-start = ((), (), s32[]{:S(2)}) async-start(), calls=%async_computation.4 | async-start | bytes 31850496 | tf_op jit(solution)/shard_map/all_gather | solution.py:57
  75.9 1.1 copy-start.7
  75.9 3.4 copy-start.8
  75.9 35.2 %copy-start.11 = (f32[1024]{0:T(1024)S(1)}, f32[1024]{0:T(1024)}, u32[]{:S(2)}) copy-start(f32[1024]{0:T(1024)} %param.10) | copy-start | bytes 12292
  118.2 3.2 copy-start.9
  118.2 5.2 copy-start.10
  118.2 611.9 %reduce-scatter.5.cloned.1.call-start = ((), (), s32[]{:S(2)}) async-start(), calls=%async_computation.3 | async-start | bytes 147456 | tf_op jit(solution)/shard_map/reduce_scatter | solution.py:98
  673.7 36.4 %copy-start = (bf16[384,768]{0,1:T(8,128)(2,1)S(1)}, bf16[384,768]{0,1:T(8,128)(2,1)}, u32[]{:S(2)}) copy-start(bf16[384,768]{0,1:T(8,128)(2,1)} %copy.15) | copy-start | bytes 1769476
  673.7 36.4 %copy-start.1 = (bf16[384,768]{0,1:T(8,128)(2,1)S(1)}, bf16[384,768]{0,1:T(8,128)(2,1)}, u32[]{:S(2)}) copy-start(bf16[384,768]{0,1:T(8,128)(2,1)} %copy.17) | copy-start | bytes 1769476
  673.7 36.4 %copy-start.2 = (bf16[384,768]{0,1:T(8,128)(2,1)S(1)}, bf16[384,768]{0,1:T(8,128)(2,1)}, u32[]{:S(2)}) copy-start(bf16[384,768]{0,1:T(8,128)(2,1)} %copy.18) | copy-start | bytes 1769476
  717.7 2.1 copy-start.5
  717.7 2.9 copy-start.6
  719.8 0.8 copy-start.3
  720.9 1.6 copy-start.4
  722.4 19.2 %reduce-scatter.3.cloned.1.call-start = ((), (), s32[]{:S(2)}) async-start(), calls=%async_computation.2 | async-start | bytes 147456 | tf_op jit(solution)/shard_map/reduce_scatter | solution.py:95
Sparse Core Ops, SparseCore 0:
  118.4 540.2 all-gather.2
  722.6 7.5 reduce-scatter.4
  732.9 8.6 reduce-scatter.2
